TPU v7x, 32 devices: a whole 2x2x4 slice. The times are simulated.
32 devices in a mesh: lat: 8 (over z, y), lon: 4 (over x, core).
Axes of the slice: x: 2, y: 2, z: 4, core: 2. Of those that a mesh axis runs over, the one named last changes fastest.
Arguments:
- pair_table: int32 [640], replicated, may hold values from 0 to 639, each once
- spectral: bfloat16 [640, 384, 1408], P('lat', 'lon'), may hold values from -0.071777344 to 0.071777344
- lat_basis: bfloat16 [640, 32, 1408], P('lat'), may hold values from -0.15625 to 0.15625
- in_weight: bfloat16 [192, 512], replicated, may hold values from -0.4375 to 0.4375
- in_bias: float32 [512], replicated, may hold values from -3 to 3
- out_weight: bfloat16 [512, 192], replicated, may hold values from -0.25 to 0.25
- out_bias: float32 [192], replicated, may hold values from -3 to 3
- cotangent: bfloat16 [64, 192, 2560], P('lat', None, 'lon'), may hold values from -0.08984375 to 0.08984375
Outputs:
- tendency: bfloat16 [64, 192, 2560], P('lat', None, 'lon')
- spectral_grad: bfloat16 [640, 384, 1408], P('lat', 'lon')
- in_weight_grad: float32 [192, 512], replicated
- in_bias_grad: float32 [512], replicated
- out_weight_grad: float32 [512, 192], replicated
- out_bias_grad: float32 [192], replicated
Inputs may be any that keep to these rules, and one draw needn't show every extreme that they name: `pair_table`: each pair number appears exactly once.
All inputs are finite; a program needn't handle non-finite values.
Results may differ from a plain program's by a relative error of at most 0.015.
Values may be sent and summed in bfloat16 or wider, within the bound.
No kernel may reach another device: no remote copies, remote signals or barrier semaphores. Data moves between devices by JAX's collectives and lax.ppermute only.
A program may use at most 256 MiB of HBM per device.

v0:
```python
import math
import jax
import jax.numpy as jnp
from jax import lax
from jax.sharding import PartitionSpec as P

TRUNC = 1279


def pair_masks(pair_ids, length):
    first_len = TRUNC + 1 - pair_ids
    position = jnp.arange(length, dtype=jnp.int32)[None, :]
    lower_part = position < first_len[:, None]
    upper_part = jnp.logical_and(position >= first_len[:, None], position < TRUNC + 2)
    offset = jnp.where(lower_part, position, position - first_len[:, None])
    parity = jnp.where(offset % 2 == 0, 1.0, -1.0).astype(jnp.float32)
    return (lower_part, upper_part, parity, first_len)


def wave_numbers(pair_ids):
    both = jnp.stack([pair_ids, TRUNC - pair_ids], axis=1)
    return both.reshape(-1)


def fourier_table(numbers, longitudes, lon_total):
    phase = numbers[:, None] * longitudes[None, :] % lon_total
    angle = phase.astype(jnp.float32) * (2.0 * math.pi / lon_total)
    factor = jnp.where(numbers == 0, 1.0, 2.0).astype(jnp.float32)[:, None]
    return jnp.stack([factor * jnp.cos(angle), -factor * jnp.sin(angle)], axis=1).astype(
        jnp.bfloat16
    )


def split_parts(coeffs, lower_part, upper_part):
    empty = jnp.zeros_like(coeffs)
    return jnp.stack(
        [
            jnp.where(lower_part[:, None, :], coeffs, empty),
            jnp.where(upper_part[:, None, :], coeffs, empty),
        ],
        axis=1,
    )


def per_device(
    pair_table, spectral, lat_basis, in_weight, in_bias, out_weight, out_bias, cotangent
):
    pair_dev = spectral.shape[0]
    width_local = spectral.shape[1]
    band_rows = cotangent.shape[0]
    block_cols = cotangent.shape[2]
    lon_total = block_cols * lax.axis_size("lon")
    first_row = lax.axis_index("lat") * pair_dev
    local_ids = lax.dynamic_slice_in_dim(pair_table, first_row, pair_dev)
    lower_part, upper_part, parity, first_len = pair_masks(local_ids, spectral.shape[2])
    mirrored = jnp.flip(lat_basis * parity[:, None, :].astype(jnp.bfloat16), axis=1)
    full_basis = jnp.concatenate([lat_basis, mirrored], axis=1)
    lat_window = full_basis.shape[1]
    masked = split_parts(spectral, lower_part, upper_part)
    waves = jnp.einsum(
        "pqkj,plj->pqlk", masked, full_basis, preferred_element_type=jnp.float32
    ).astype(jnp.bfloat16)
    flat_waves = waves.reshape(2 * pair_dev, lat_window * width_local)
    band_waves = lax.all_to_all(flat_waves, "lat", split_axis=1, concat_axis=0, tiled=True)
    wave_count = band_waves.shape[0]
    coeff_grid = band_waves.reshape(wave_count, band_rows, width_local // 2, 2)
    numbers = wave_numbers(pair_table)
    full_table = fourier_table(numbers, jnp.arange(lon_total, dtype=jnp.int32), lon_total)
    all_columns = jnp.einsum(
        "glkc,gcn->lkn", coeff_grid, full_table, preferred_element_type=jnp.float32
    ).astype(jnp.bfloat16)
    grid = lax.all_to_all(all_columns, "lon", split_axis=2, concat_axis=1, tiled=True)
    pre_act = (
        jnp.einsum("lkc,kh->lch", grid, in_weight, preferred_element_type=jnp.float32) + in_bias
    )
    activated, gelu_back = jax.vjp(jax.nn.gelu, pre_act)
    hidden = activated.astype(jnp.bfloat16)
    tendency = (
        jnp.einsum("lch,hk->lkc", hidden, out_weight, preferred_element_type=jnp.float32)
        + out_bias[None, :, None]
    ).astype(jnp.bfloat16)
    out_weight_part = jnp.einsum(
        "lch,lkc->hk", hidden, cotangent, preferred_element_type=jnp.float32
    )
    out_bias_part = jnp.sum(cotangent.astype(jnp.float32), axis=(0, 2))
    hidden_grad = jnp.einsum(
        "lkc,hk->lch", cotangent, out_weight, preferred_element_type=jnp.float32
    )
    pre_grad = gelu_back(hidden_grad)[0].astype(jnp.bfloat16)
    in_weight_part = jnp.einsum("lkc,lch->kh", grid, pre_grad, preferred_element_type=jnp.float32)
    in_bias_part = jnp.sum(pre_grad.astype(jnp.float32), axis=(0, 1))
    grid_grad = jnp.einsum(
        "lch,kh->lkc", pre_grad, in_weight, preferred_element_type=jnp.float32
    ).astype(jnp.bfloat16)
    in_weight_grad, in_bias_grad, out_weight_grad, out_bias_grad = lax.psum(
        (in_weight_part, in_bias_part, out_weight_part, out_bias_part), ("lat", "lon")
    )
    level_rows = lax.all_to_all(grid_grad, "lon", split_axis=1, concat_axis=2, tiled=True)
    wave_grad = jnp.einsum(
        "gcn,lkn->glkc", full_table, level_rows, preferred_element_type=jnp.float32
    ).astype(jnp.bfloat16)
    flat_grad = wave_grad.reshape(wave_count, band_rows * width_local)
    pair_grad = lax.all_to_all(flat_grad, "lat", split_axis=0, concat_axis=1, tiled=True)
    pair_grad = pair_grad.reshape(pair_dev, 2, lat_window, width_local)
    contrib = jnp.einsum(
        "pqlk,plj->pqkj", pair_grad, full_basis, preferred_element_type=jnp.float32
    )
    empty = jnp.zeros_like(contrib[:, 0])
    spectral_grad = (
        jnp.where(lower_part[:, None, :], contrib[:, 0], empty)
        + jnp.where(upper_part[:, None, :], contrib[:, 1], empty)
    ).astype(jnp.bfloat16)
    return (tendency, spectral_grad, in_weight_grad, in_bias_grad, out_weight_grad, out_bias_grad)


def solution(mesh):
    placed = (
        P(),
        P("lat", "lon", None),
        P("lat", None, None),
        P(),
        P(),
        P(),
        P(),
        P("lat", None, "lon"),
    )
    return jax.shard_map(
        per_device,
        mesh=mesh,
        in_specs=placed,
        out_specs=(P("lat", None, "lon"), P("lat", "lon", None), P(), P(), P(), P()),
        check_vma=False,
    )
```

profile of v0, /device:TPU:0, one launch (start us, length us, event | category | flops | bytes accessed | tf_op | source)
XLA Modules:
  0.0 471.3 jit_solution(12344877415564866981)
XLA Ops:
  8.6 7.0 %broadcast_multiply_fusion = bf16[80,32,1408]{2,1,0:T(8,128)(2,1)} fusion(bf16[80,32,1408]{2,1,0:T(8,128)(2,1)} %param.10, bf16[80,1408]{1,0:T(8,128)(2,1)S(1)} %select_convert_fusion), kind=kLoop, calls=%fused_computation.43 | loop fusion | flops 3604480 | bytes 14643200 | tf_op jit(solution)/shard_map/mul | solution.py:56
  15.6 20.3 %rev.4 = bf16[80,32,1408]{2,1,0:T(8,128)(2,1)} reverse(bf16[80,32,1408]{2,1,0:T(8,128)(2,1)} %broadcast_multiply_fusion), dimensions={1} | reverse | bytes 14417920 | tf_op jit(solution)/shard_map/jit(_flip)/rev | solution.py:56
  35.9 23.5 %select_bitcast_fusion.1 = (bf16[80,1,96,1408]{3,2,1,0:T(8,128)(2,1)}, bf16[80,1,96,1408]{3,2,1,0:T(8,128)(2,1)}) fusion(bf16[80,96,1408]{2,1,0:T(8,128)(2,1)} %param.9, pred[80,1408]{1,0:T(8,128)(4,1)S(1)} %get-tuple-element.16, pred[80,1408]{1,0:T(8,128)(4,1)S(1)} %get-tuple-element.17), kind=kLoop, calls=%fused_computation.11 | loop fusion | flops 21626880 | bytes 65105920 | tf_op jit(solution)/shard_map/stack | solution.py:36
  59.4 24.7 %convert_bitcast_fusion = bf16[80,2,64,96]{3,2,1,0:T(8,128)(2,1)} fusion(bf16[80,1,96,1408]{3,2,1,0:T(8,128)(2,1)} %get-tuple-element.11, bf16[80,1,96,1408]{3,2,1,0:T(8,128)(2,1)} %get-tuple-element.10, bf16[80,32,1408]{2,1,0:T(8,128)(2,1)} %rev.4, bf16[80,32,1408]{2,1,0:T(8,128)(2,1)} %param.10), kind=kOutput, calls=%fused_computation.47 | convolution fusion | flops 2884567040 | bytes 59637760 | tf_op jit(solution)/shard_map/pqkj,plj->pqlk/dot_general | solution.py:60
  90.1 7.6 %all-to-all-start = ((bf16[160,8,768]{2,0,1:T(8,128)(2,1)}), bf16[160,8,768]{2,0,1:T(8,128)(2,1)S(1)}, u32[]{:S(2)}, u32[]{:S(2)}) async-start(bf16[160,8,768]{2,0,1:T(8,128)(2,1)} %copy.30), calls=%async_computation | async-start | bytes 3932160 | tf_op jit(solution)/shard_map/all_to_all | solution.py:64
  98.2 58.1 %multiply_convert_fusion.1 = (bf16[1280,1,2560]{2,0,1:T(8,128)(2,1)}, bf16[1280,1,2560]{2,0,1:T(8,128)(2,1)}) fusion(s32[1280]{0:T(1024)S(1)} %reshape.286, f32[1280]{0:T(1024)S(1)} %get-tuple-element.14, f32[1280]{0:T(1024)S(1)} %get-tuple-element.15), kind=kLoop, calls=%fused_computation.23 | loop fusion | flops 42598400 | bytes 13122560 | tf_op jit(solution)/shard_map/convert
  161.6 5.2 %reshape.285 = bf16[1280,8,48,2]{0,3,2,1:T(2,128)(2,1)} reshape(bf16[8,160,768]{1,0,2:T(8,128)(2,1)S(1)} %copy.31) | data formatting | bytes 3932160 | tf_op jit(solution)/shard_map/reshape | solution.py:66
  166.9 9.0 %fusion.26 = bf16[8,48,2560]{2,1,0:T(8,128)(2,1)S(1)} fusion(bf16[1280,1,2560]{2,0,1:T(8,128)(2,1)} %get-tuple-element.13, bf16[1280,1,2560]{2,0,1:T(8,128)(2,1)} %get-tuple-element.12, bf16[1280,8,48,2]{0,3,2,1:T(2,128)(2,1)} %reshape.285), kind=kOutput, calls=%fused_computation.40 | convolution fusion | flops 5040701440 | bytes 17039360 | tf_op jit(solution)/shard_map/glkc,gcn->lkn/dot_general | solution.py:69
  175.9 5.2 %copy.34 = bf16[8,48,2560]{1,0,2:T(8,128)(2,1)} copy(bf16[8,48,2560]{2,1,0:T(8,128)(2,1)S(1)} %fusion.26) | data formatting | bytes 3932160 | tf_op jit(solution)/shard_map/convert_element_type | solution.py:71
  181.1 8.8 %reshape.297 = bf16[4,2,122880]{2,1,0:T(2,128)(2,1)S(1)} reshape(bf16[2560,8,48]{2,1,0:T(8,128)(2,1)} %bitcast.101) | data formatting | bytes 3932160
  190.0 28.0 %all_to_all.68 = bf16[4,2,122880]{2,1,0:T(2,128)(2,1)} all-to-all(bf16[4,2,122880]{2,1,0:T(2,128)(2,1)S(1)} %reshape.297), channel_id=1, replica_groups=mesh['lat'=8,'lon'=4] {'lon'}, dimensions={0} | all-to-all | bytes 3932160 | tf_op jit(solution)/shard_map/all_to_all | solution.py:72
  218.0 7.0 %reshape.298 = bf16[2560,8,48]{2,1,0:T(8,128)(2,1)} reshape(bf16[4,2,122880]{2,1,0:T(2,128)(2,1)} %all_to_all.68) | data formatting | bytes 3932160
  225.0 5.7 %copy.35 = bf16[8,48,4,640]{3,1,2,0:T(8,128)(2,1)S(1)} copy(bf16[8,48,4,640]{1,0,3,2:T(8,128)(2,1)} %bitcast.102) | data formatting | bytes 3932160 | tf_op jit(solution)/shard_map/all_to_all | solution.py:72
  230.8 5.5 %multiply_convert_fusion.2 = (bf16[8,640,512]{2,1,0:T(8,128)(2,1)}, f32[8,640,512]{2,1,0:T(8,128)S(1)}) fusion(f32[512]{0:T(512)S(1)} %copy-done.13, bf16[8,192,640]{2,1,0:T(8,128)(2,1)S(1)} %bitcast.107, bf16[192,512]{1,0:T(8,128)(2,1)S(1)} %copy-done), kind=kOutput, calls=%fused_computation.36 | convolution fusion | flops 1032847360 | bytes 17893376 | tf_op jit(solution)/shard_map/lkc,kh->lch/dot_general | solution.py:74
  236.3 8.7 %convert_reduce_fusion = (f32[512]{0:T(512)S(1)}, bf16[8,640,512]{2,1,0:T(8,128)(2,1)S(1)}) fusion(f32[8,640,512]{2,1,0:T(8,128)S(1)} %get-tuple-element.19, f32[512]{0:T(512)S(1)} %copy-done.13, bf16[8,192,640]{2,1,0:T(8,128)(2,1)S(1)} %copy-done.4, bf16[512,192]{0,1:T(8,128)(2,1)S(1)} %copy-done.12), kind=kOutput, calls=%fused_computation.35 | convolution fusion | flops 1066925568 | bytes 17895424 | tf_op jit(solution)/shard_map/lkc,hk->lch/dot_general | solution.py:86
  248.0 26.9 %all_to_all.69 = bf16[8,192,640]{2,0,1:T(8,128)(2,1)S(1)} all-to-all(bf16[8,192,640]{2,0,1:T(8,128)(2,1)S(1)} %copy.36), channel_id=1, replica_groups=mesh['lat'=8,'lon'=4] {'lon'}, dimensions={1} | all-to-all | bytes 3932160 | tf_op jit(solution)/shard_map/all_to_all | solution.py:98
  278.6 9.0 %fusion.28 = bf16[1280,8,48,2]{0,2,3,1:T(8,128)(2,1)S(1)} fusion(bf16[1280,1,2560]{2,0,1:T(8,128)(2,1)} %get-tuple-element.13, bf16[1280,1,2560]{2,0,1:T(8,128)(2,1)} %get-tuple-element.12, bf16[8,48,2560,1]{2,1,0,3:T(8,128)(2,1)} %reshape.293), kind=kOutput, calls=%fused_computation.45 | convolution fusion | flops 5060362240 | bytes 17039360 | tf_op jit(solution)/shard_map/gcn,lkn->glkc/dot_general | solution.py:99
  290.4 6.4 %all_to_all.61 = bf16[8,160,768]{1,0,2:T(8,128)(2,1)S(1)} reshape(bf16[1280,8,48,2]{0,3,2,1:T(2,128)(2,1)} %copy.38) | data formatting | bytes 3932160 | tf_op jit(solution)/shard_map/all_to_all | solution.py:103
  300.1 6.0 %all-to-all-start.3 = ((bf16[8,160,768]{2,1,0:T(8,128)(2,1)}), bf16[8,160,768]{2,1,0:T(8,128)(2,1)S(1)}, u32[]{:S(2)}, u32[]{:S(2)}) async-start(bf16[8,160,768]{2,1,0:T(8,128)(2,1)} %copy.39), calls=%async_computation.3 | async-start | bytes 3932160 | tf_op jit(solution)/shard_map/all_to_all | solution.py:103
  308.2 5.0 %convolution_bitcast_fusion.1 = f32[192,512]{1,0:T(8,128)} fusion(bf16[8,192,640]{2,1,0:T(8,128)(2,1)} %bitcast.108, bf16[8,640,512]{2,1,0:T(8,128)(2,1)} %copy-done.3), kind=kOutput, calls=%fused_computation.54 | convolution fusion | flops 1006632960 | bytes 7602176 | tf_op jit(solution)/shard_map/lkc,lch->kh/dot_general | solution.py:90
  317.7 56.7 %all-reduce = (f32[512]{0:T(512)}, f32[192]{0:T(256)}) all-reduce(f32[512]{0:T(512)S(1)} %get-tuple-element.20, f32[192]{0:T(256)S(1)} %convert_reduce_fusion.1), channel_id=1, replica_groups=mesh['lat'=8,'lon'=4] {'lat','lon'}, use_global_device_ids=true, to_apply=%region_2.3 | all-reduce | flops 704 | bytes 5632 | tf_op jit(solution)/shard_map/psum | solution.py:95
  374.4 5.7 %fusion.36 = bf16[8,192,640]{2,1,0:T(8,128)(2,1)} fusion(f32[192]{0:T(256)S(1)} %copy-done.14, bf16[8,640,512]{2,1,0:T(8,128)(2,1)} %get-tuple-element.18, bf16[512,192]{0,1:T(8,128)(2,1)S(1)} %copy-done.12), kind=kOutput, calls=%fused_computation.52 | convolution fusion | flops 1008599040 | bytes 7406336 | tf_op jit(solution)/shard_map/lch,hk->lkc/dot_general | solution.py:79
  387.0 34.6 %fusion.9 = f32[80,2,96,1408]{3,2,0,1:T(8,128)} fusion(bf16[80,32,1408]{2,1,0:T(8,128)(2,1)} %rev.4, bf16[80,32,1408]{2,1,0:T(8,128)(2,1)} %param.10, bf16[80,2,64,96]{3,2,1,0:T(8,128)(2,1)S(1)} %reshape.287), kind=kOutput, calls=%fused_computation.17 | convolution fusion | flops 2797076480 | bytes 102891520 | tf_op jit(solution)/shard_map/pqlk,plj->pqkj/dot_general | solution.py:105
  421.6 36.2 %fusion.2 = bf16[80,96,1408]{2,1,0:T(8,128)(2,1)} fusion(f32[80,2,96,1408]{3,2,0,1:T(8,128)} %fusion.9, pred[80,1408]{1,0:T(8,128)(4,1)S(1)} %copy-done.10, pred[80,1408]{1,0:T(8,128)(4,1)S(1)} %copy-done.8), kind=kLoop, calls=%fused_computation.3 | loop fusion | flops 43253760 | bytes 108359680 | tf_op jit(solution)/shard_map/convert_element_type | solution.py:112
  (61 shorter events, 45.7 us)
Async XLA Ops:
  7.2 223.6 %copy-start = (bf16[192,512]{1,0:T(8,128)(2,1)S(1)}, bf16[192,512]{1,0:T(8,128)(2,1)}, u32[]{:S(2)}) copy-start(bf16[192,512]{1,0:T(8,128)(2,1)} %param.11) | copy-start | bytes 589828
  8.6 27.4 %copy-start.7 = (pred[80,1408]{1,0:T(8,128)(4,1)}, pred[80,1408]{1,0:T(8,128)(4,1)S(1)}, u32[]{:S(2)}) copy-start(pred[80,1408]{1,0:T(8,128)(4,1)S(1)} %get-tuple-element.16) | copy-start | bytes 337924
  8.6 27.4 %copy-start.9 = (pred[80,1408]{1,0:T(8,128)(4,1)}, pred[80,1408]{1,0:T(8,128)(4,1)S(1)}, u32[]{:S(2)}) copy-start(pred[80,1408]{1,0:T(8,128)(4,1)S(1)} %get-tuple-element.17) | copy-start | bytes 337924
  84.1 13.6 %copy-start.11 = (s32[640]{0:T(1024)S(1)}, s32[640]{0:T(1024)}, u32[]{:S(2)}) copy-start(s32[640]{0:T(1024)} %param.8) | copy-start | bytes 7684
  90.1 66.2 %all-to-all-start = ((bf16[160,8,768]{2,0,1:T(8,128)(2,1)}), bf16[160,8,768]{2,0,1:T(8,128)(2,1)S(1)}, u32[]{:S(2)}, u32[]{:S(2)}) async-start(bf16[160,8,768]{2,0,1:T(8,128)(2,1)} %copy.30), calls=%async_computation | async-start | bytes 3932160 | tf_op jit(solution)/shard_map/all_to_all | solution.py:64
  156.3 1.3 copy-start.2
  189.9 40.8 %copy-start.13 = (f32[512]{0:T(512)S(1)}, f32[512]{0:T(512)}, u32[]{:S(2)}) copy-start(f32[512]{0:T(512)} %param.12) | copy-start | bytes 6148
  230.8 5.5 %copy-start.6 = (bf16[8,48,4,640]{3,1,2,0:T(8,128)(2,1)}, bf16[8,48,4,640]{3,1,2,0:T(8,128)(2,1)S(1)}, u32[]{:S(2)}) copy-start(bf16[8,48,4,640]{3,1,2,0:T(8,128)(2,1)S(1)} %copy.35) | copy-start | bytes 5898244
  230.8 5.5 %copy-start.4 = (bf16[8,192,640]{2,1,0:T(8,128)(2,1)S(1)}, bf16[8,192,640]{2,1,0:T(8,128)(2,1)}, u32[]{:S(2)}) copy-start(bf16[8,192,640]{2,1,0:T(8,128)(2,1)} %param.15) | copy-start | bytes 5898244
  230.8 5.5 %copy-start.12 = (bf16[512,192]{0,1:T(8,128)(2,1)S(1)}, bf16[512,192]{0,1:T(8,128)(2,1)}, u32[]{:S(2)}) copy-start(bf16[512,192]{0,1:T(8,128)(2,1)} %param.13) | copy-start | bytes 589828
  245.0 31.4 %copy-start.3 = (bf16[8,640,512]{2,1,0:T(8,128)(2,1)}, bf16[8,640,512]{2,1,0:T(8,128)(2,1)S(1)}, u32[]{:S(2)}) copy-start(bf16[8,640,512]{2,1,0:T(8,128)(2,1)S(1)} %get-tuple-element.21) | copy-start | bytes 15728644
  300.1 80.0 %all-to-all-start.3 = ((bf16[8,160,768]{2,1,0:T(8,128)(2,1)}), bf16[8,160,768]{2,1,0:T(8,128)(2,1)S(1)}, u32[]{:S(2)}, u32[]{:S(2)}) async-start(bf16[8,160,768]{2,1,0:T(8,128)(2,1)} %copy.39), calls=%async_computation.3 | async-start | bytes 3932160 | tf_op jit(solution)/shard_map/all_to_all | solution.py:103
  306.1 154.6 %all-reduce.4.cloned.1.call-start = ((), (), s32[]{:S(2)}) async-start(), calls=%async_computation.4 | async-start | bytes 1572864 | tf_op jit(solution)/shard_map/psum | solution.py:95
  306.1 7.1 %copy-start.5 = (bf16[8,192,640]{2,1,0:T(8,128)(2,1)S(1)}, bf16[8,192,640]{2,1,0:T(8,128)(2,1)}, u32[]{:S(2)}) copy-start(bf16[8,192,640]{2,1,0:T(8,128)(2,1)} %param.15) | copy-start | bytes 5898244
  308.2 66.2 %copy-start.14 = (f32[192]{0:T(256)S(1)}, f32[192]{0:T(256)}, u32[]{:S(2)}) copy-start(f32[192]{0:T(256)} %param.14) | copy-start | bytes 2308
  387.0 34.6 %copy-start.8 = (pred[80,1408]{1,0:T(8,128)(4,1)S(1)}, pred[80,1408]{1,0:T(8,128)(4,1)}, u32[]{:S(2)}) copy-start(pred[80,1408]{1,0:T(8,128)(4,1)} %copy-done.7) | copy-start | bytes 337924
  387.0 34.6 %copy-start.10 = (pred[80,1408]{1,0:T(8,128)(4,1)S(1)}, pred[80,1408]{1,0:T(8,128)(4,1)}, u32[]{:S(2)}) copy-start(pred[80,1408]{1,0:T(8,128)(4,1)} %copy-done.9) | copy-start | bytes 337924
  421.6 42.6 %copy-start.1 = (bf16[192,512]{1,0:T(8,128)(2,1)S(1)}, bf16[192,512]{1,0:T(8,128)(2,1)}, u32[]{:S(2)}) copy-start(bf16[192,512]{1,0:T(8,128)(2,1)} %param.11) | copy-start | bytes 589828
Sparse Core Ops, SparseCore 0:
  317.8 142.8 all-reduce.3
where the time goes:
time: 477 us; the launch traced here: 471 us
  other arithmetic  128 us (27%)
  blocking collectives  112 us (23%)
  matrix products  108 us (23%)
  local copies, waits for them, and re-layouts  91.9 us (19%)
  between operations  14.6 us (3%)
  starting transfers between devices  13.6 us (3%)
    another operation x1, other arithmetic  58.1 us
    psum x1, blocking collectives, per_device(): lax.psum((in_weight_part, in_bias_part, out_weight_part, out_bias_part),...  56.7 us
    convert_element_type x1, other arithmetic, per_device(): spectral_grad = (jnp.where(lower_part[:, None, :], contrib[:, 0], empty)...  36.2 us
    dot_general x1, matrix products, per_device(): jnp.einsum('pqlk,plj->pqkj', pair_grad, full_basis, preferred_element_typ...  34.6 us
    all_to_all x1, blocking collectives, per_device(): lax.all_to_all(all_columns, 'lon', split_axis=2, concat_axis=1, tiled=True)  28 us
    all_to_all x1, blocking collectives, per_device(): lax.all_to_all(grid_grad, 'lon', split_axis=1, concat_axis=2, tiled=True)  26.9 us
    dot_general x1, matrix products, per_device(): jnp.einsum('pqkj,plj->pqlk', masked, full_basis, preferred_element_type=j...  24.7 us
    another operation x1, other arithmetic, split_parts(): jnp.stack([jnp.where(lower_part[:, None, :], coeffs, empty), jnp.where(up...  23.5 us
  transfers between devices with their start and end apart: 3, of which 1 were waited for; matrix products, arithmetic and copies ran while one was open for 33% of the time, Pallas kernels for 0%

commit v1 on v0

--- a/solution.py
+++ b/solution.py
@@ -93,7 +93,7 @@
         "lch,kh->lkc", pre_grad, in_weight, preferred_element_type=jnp.float32
     ).astype(jnp.bfloat16)
     in_weight_grad, in_bias_grad, out_weight_grad, out_bias_grad = lax.psum(
-        (in_weight_part, in_bias_part, out_weight_part, out_bias_part), ("lat", "lon")
+        lax.psum((in_weight_part, in_bias_part, out_weight_part, out_bias_part), "lon"), "lat"
     )
     level_rows = lax.all_to_all(grid_grad, "lon", split_axis=1, concat_axis=2, tiled=True)
     wave_grad = jnp.einsum(

time: 477 us -> 458 us (0.960)
  blocking collectives: 112 us -> 91 us
    psum x1, blocking collectives: 56.7 us -> 5.96 us  [per_device(): lax.psum((in_weight_part, in_bias_part, out_weight_part, out_bias_part),...]
    psum x0 -> x1, blocking collectives: none -> 30 us  [per_device(): lax.psum(lax.psum((in_weight_part, in_bias_part, out_weight_part, out_bia...]
  transfers between devices with their start and end apart: 3 -> 4, of which waited for: 1 -> 1; matrix products, arithmetic and copies ran while one was open for 33% -> 34% of each run, Pallas kernels for 0% -> 0%
where the time goes in v1:
time: 458 us; the launch traced here: 450 us
  other arithmetic  128 us (28%)
  matrix products  108 us (24%)
  local copies, waits for them, and re-layouts  91.9 us (20%)
  blocking collectives  91 us (20%)
  between operations  14.6 us (3%)
  starting transfers between devices  13.7 us (3%)
    another operation x1, other arithmetic  58.1 us
    convert_element_type x1, other arithmetic, per_device(): spectral_grad = (jnp.where(lower_part[:, None, :], contrib[:, 0], empty)...  36.3 us
    dot_general x1, matrix products, per_device(): jnp.einsum('pqlk,plj->pqkj', pair_grad, full_basis, preferred_element_typ...  34.7 us
    psum x1, blocking collectives, per_device(): lax.psum(lax.psum((in_weight_part, in_bias_part, out_weight_part, out_bia...  30 us
    all_to_all x1, blocking collectives, per_device(): lax.all_to_all(all_columns, 'lon', split_axis=2, concat_axis=1, tiled=True)  28 us
    all_to_all x1, blocking collectives, per_device(): lax.all_to_all(grid_grad, 'lon', split_axis=1, concat_axis=2, tiled=True)  26.9 us
    dot_general x1, matrix products, per_device(): jnp.einsum('pqkj,plj->pqlk', masked, full_basis, preferred_element_type=j...  24.7 us
    another operation x1, other arithmetic, split_parts(): jnp.stack([jnp.where(lower_part[:, None, :], coeffs, empty), jnp.where(up...  23.5 us
  transfers between devices with their start and end apart: 4, of which 1 were waited for; matrix products, arithmetic and copies ran while one was open for 34% of the time, Pallas kernels for 0%

profile of v1, /device:TPU:0, one launch (start us, length us, event | category | flops | bytes accessed | tf_op | source)
XLA Modules:
  0.0 449.7 jit_solution(7989691860063467664)
XLA Ops:
  8.6 7.0 %broadcast_multiply_fusion = bf16[80,32,1408]{2,1,0:T(8,128)(2,1)} fusion(bf16[80,32,1408]{2,1,0:T(8,128)(2,1)} %param.10, bf16[80,1408]{1,0:T(8,128)(2,1)S(1)} %select_convert_fusion), kind=kLoop, calls=%fused_computation.43 | loop fusion | flops 3604480 | bytes 14643200 | tf_op jit(solution)/shard_map/mul | solution.py:56
  15.6 20.3 %rev.4 = bf16[80,32,1408]{2,1,0:T(8,128)(2,1)} reverse(bf16[80,32,1408]{2,1,0:T(8,128)(2,1)} %broadcast_multiply_fusion), dimensions={1} | reverse | bytes 14417920 | tf_op jit(solution)/shard_map/jit(_flip)/rev | solution.py:56
  35.9 23.5 %select_bitcast_fusion.1 = (bf16[80,1,96,1408]{3,2,1,0:T(8,128)(2,1)}, bf16[80,1,96,1408]{3,2,1,0:T(8,128)(2,1)}) fusion(bf16[80,96,1408]{2,1,0:T(8,128)(2,1)} %param.9, pred[80,1408]{1,0:T(8,128)(4,1)S(1)} %get-tuple-element.20, pred[80,1408]{1,0:T(8,128)(4,1)S(1)} %get-tuple-element.21), kind=kLoop, calls=%fused_computation.11 | loop fusion | flops 21626880 | bytes 65105920 | tf_op jit(solution)/shard_map/stack | solution.py:36
  59.4 24.7 %convert_bitcast_fusion = bf16[80,2,64,96]{3,2,1,0:T(8,128)(2,1)} fusion(bf16[80,1,96,1408]{3,2,1,0:T(8,128)(2,1)} %get-tuple-element.15, bf16[80,1,96,1408]{3,2,1,0:T(8,128)(2,1)} %get-tuple-element.14, bf16[80,32,1408]{2,1,0:T(8,128)(2,1)} %rev.4, bf16[80,32,1408]{2,1,0:T(8,128)(2,1)} %param.10), kind=kOutput, calls=%fused_computation.47 | convolution fusion | flops 2884567040 | bytes 59637760 | tf_op jit(solution)/shard_map/pqkj,plj->pqlk/dot_general | solution.py:60
  90.1 7.6 %all-to-all-start = ((bf16[160,8,768]{2,0,1:T(8,128)(2,1)}), bf16[160,8,768]{2,0,1:T(8,128)(2,1)S(1)}, u32[]{:S(2)}, u32[]{:S(2)}) async-start(bf16[160,8,768]{2,0,1:T(8,128)(2,1)} %copy.30), calls=%async_computation | async-start | bytes 3932160 | tf_op jit(solution)/shard_map/all_to_all | solution.py:64
  98.2 58.1 %multiply_convert_fusion.1 = (bf16[1280,1,2560]{2,0,1:T(8,128)(2,1)}, bf16[1280,1,2560]{2,0,1:T(8,128)(2,1)}) fusion(s32[1280]{0:T(1024)S(1)} %reshape.286, f32[1280]{0:T(1024)S(1)} %get-tuple-element.18, f32[1280]{0:T(1024)S(1)} %get-tuple-element.19), kind=kLoop, calls=%fused_computation.23 | loop fusion | flops 42598400 | bytes 13122560 | tf_op jit(solution)/shard_map/convert
  161.6 5.2 %reshape.285 = bf16[1280,8,48,2]{0,3,2,1:T(2,128)(2,1)} reshape(bf16[8,160,768]{1,0,2:T(8,128)(2,1)S(1)} %copy.31) | data formatting | bytes 3932160 | tf_op jit(solution)/shard_map/reshape | solution.py:66
  166.9 9.0 %fusion.26 = bf16[8,48,2560]{2,1,0:T(8,128)(2,1)S(1)} fusion(bf16[1280,1,2560]{2,0,1:T(8,128)(2,1)} %get-tuple-element.17, bf16[1280,1,2560]{2,0,1:T(8,128)(2,1)} %get-tuple-element.16, bf16[1280,8,48,2]{0,3,2,1:T(2,128)(2,1)} %reshape.285), kind=kOutput, calls=%fused_computation.40 | convolution fusion | flops 5040701440 | bytes 17039360 | tf_op jit(solution)/shard_map/glkc,gcn->lkn/dot_general | solution.py:69
  175.9 5.2 %copy.34 = bf16[8,48,2560]{1,0,2:T(8,128)(2,1)} copy(bf16[8,48,2560]{2,1,0:T(8,128)(2,1)S(1)} %fusion.26) | data formatting | bytes 3932160 | tf_op jit(solution)/shard_map/convert_element_type | solution.py:71
  181.1 8.8 %reshape.297 = bf16[4,2,122880]{2,1,0:T(2,128)(2,1)S(1)} reshape(bf16[2560,8,48]{2,1,0:T(8,128)(2,1)} %bitcast.101) | data formatting | bytes 3932160
  190.0 28.0 %all_to_all.68 = bf16[4,2,122880]{2,1,0:T(2,128)(2,1)} all-to-all(bf16[4,2,122880]{2,1,0:T(2,128)(2,1)S(1)} %reshape.297), channel_id=1, replica_groups=mesh['lat'=8,'lon'=4] {'lon'}, dimensions={0} | all-to-all | bytes 3932160 | tf_op jit(solution)/shard_map/all_to_all | solution.py:72
  218.0 7.0 %reshape.298 = bf16[2560,8,48]{2,1,0:T(8,128)(2,1)} reshape(bf16[4,2,122880]{2,1,0:T(2,128)(2,1)} %all_to_all.68) | data formatting | bytes 3932160
  225.0 5.7 %copy.35 = bf16[8,48,4,640]{3,1,2,0:T(8,128)(2,1)S(1)} copy(bf16[8,48,4,640]{1,0,3,2:T(8,128)(2,1)} %bitcast.102) | data formatting | bytes 3932160 | tf_op jit(solution)/shard_map/all_to_all | solution.py:72
  230.8 5.5 %multiply_convert_fusion.2 = (bf16[8,640,512]{2,1,0:T(8,128)(2,1)}, f32[8,640,512]{2,1,0:T(8,128)S(1)}) fusion(f32[512]{0:T(512)S(1)} %copy-done.13, bf16[8,192,640]{2,1,0:T(8,128)(2,1)S(1)} %bitcast.107, bf16[192,512]{1,0:T(8,128)(2,1)S(1)} %copy-done), kind=kOutput, calls=%fused_computation.36 | convolution fusion | flops 1032847360 | bytes 17893376 | tf_op jit(solution)/shard_map/lkc,kh->lch/dot_general | solution.py:74
  236.3 8.7 %convert_reduce_fusion = (f32[512]{0:T(512)S(1)}, bf16[8,640,512]{2,1,0:T(8,128)(2,1)S(1)}) fusion(f32[8,640,512]{2,1,0:T(8,128)S(1)} %get-tuple-element.23, f32[512]{0:T(512)S(1)} %copy-done.13, bf16[8,192,640]{2,1,0:T(8,128)(2,1)S(1)} %copy-done.4, bf16[512,192]{0,1:T(8,128)(2,1)S(1)} %copy-done.12), kind=kOutput, calls=%fused_computation.35 | convolution fusion | flops 1066925568 | bytes 17895424 | tf_op jit(solution)/shard_map/lkc,hk->lch/dot_general | solution.py:86
  248.0 26.9 %all_to_all.69 = bf16[8,192,640]{2,0,1:T(8,128)(2,1)S(1)} all-to-all(bf16[8,192,640]{2,0,1:T(8,128)(2,1)S(1)} %copy.36), channel_id=1, replica_groups=mesh['lat'=8,'lon'=4] {'lon'}, dimensions={1} | all-to-all | bytes 3932160 | tf_op jit(solution)/shard_map/all_to_all | solution.py:98
  278.6 9.0 %fusion.28 = bf16[1280,8,48,2]{0,2,3,1:T(8,128)(2,1)S(1)} fusion(bf16[1280,1,2560]{2,0,1:T(8,128)(2,1)} %get-tuple-element.17, bf16[1280,1,2560]{2,0,1:T(8,128)(2,1)} %get-tuple-element.16, bf16[8,48,2560,1]{2,1,0,3:T(8,128)(2,1)} %reshape.293), kind=kOutput, calls=%fused_computation.45 | convolution fusion | flops 5060362240 | bytes 17039360 | tf_op jit(solution)/shard_map/gcn,lkn->glkc/dot_general | solution.py:99
  290.4 6.4 %all_to_all.61 = bf16[8,160,768]{1,0,2:T(8,128)(2,1)S(1)} reshape(bf16[1280,8,48,2]{0,3,2,1:T(2,128)(2,1)} %copy.38) | data formatting | bytes 3932160 | tf_op jit(solution)/shard_map/all_to_all | solution.py:103
  300.1 6.0 %all-to-all-start.3 = ((bf16[8,160,768]{2,1,0:T(8,128)(2,1)}), bf16[8,160,768]{2,1,0:T(8,128)(2,1)S(1)}, u32[]{:S(2)}, u32[]{:S(2)}) async-start(bf16[8,160,768]{2,1,0:T(8,128)(2,1)} %copy.39), calls=%async_computation.3 | async-start | bytes 3932160 | tf_op jit(solution)/shard_map/all_to_all | solution.py:103
  317.7 6.0 %all-reduce.2 = (f32[512]{0:T(512)S(1)}, f32[192]{0:T(256)S(1)}) all-reduce(f32[512]{0:T(512)S(1)} %get-tuple-element.24, f32[192]{0:T(256)S(1)} %convert_reduce_fusion.1), channel_id=1, replica_groups=mesh['lat'=8,'lon'=4] {'lon'}, use_global_device_ids=true, to_apply=%region_3.4 | all-reduce | flops 704 | bytes 5632 | tf_op jit(solution)/shard_map/psum | solution.py:96
  323.7 30.0 %all-reduce = (f32[512]{0:T(512)}, f32[192]{0:T(256)}) all-reduce(f32[512]{0:T(512)S(1)} %get-tuple-element.10, f32[192]{0:T(256)S(1)} %get-tuple-element.11), channel_id=1, replica_groups=mesh['lat'=8,'lon'=4] {'lat'}, use_global_device_ids=true, to_apply=%region_4.5 | all-reduce | flops 704 | bytes 5632 | tf_op jit(solution)/shard_map/psum | solution.py:95
  353.7 5.6 %fusion.36 = bf16[8,192,640]{2,1,0:T(8,128)(2,1)} fusion(f32[192]{0:T(256)S(1)} %copy-done.14, bf16[8,640,512]{2,1,0:T(8,128)(2,1)} %get-tuple-element.22, bf16[512,192]{0,1:T(8,128)(2,1)S(1)} %copy-done.12), kind=kOutput, calls=%fused_computation.52 | convolution fusion | flops 1008599040 | bytes 7406336 | tf_op jit(solution)/shard_map/lch,hk->lkc/dot_general | solution.py:79
  366.3 34.7 %fusion.9 = f32[80,2,96,1408]{3,2,0,1:T(8,128)} fusion(bf16[80,32,1408]{2,1,0:T(8,128)(2,1)} %rev.4, bf16[80,32,1408]{2,1,0:T(8,128)(2,1)} %param.10, bf16[80,2,64,96]{3,2,1,0:T(8,128)(2,1)S(1)} %reshape.287), kind=kOutput, calls=%fused_computation.17 | convolution fusion | flops 2797076480 | bytes 102891520 | tf_op jit(solution)/shard_map/pqlk,plj->pqkj/dot_general | solution.py:105
  401.1 36.3 %fusion.2 = bf16[80,96,1408]{2,1,0:T(8,128)(2,1)} fusion(f32[80,2,96,1408]{3,2,0,1:T(8,128)} %fusion.9, pred[80,1408]{1,0:T(8,128)(4,1)S(1)} %copy-done.10, pred[80,1408]{1,0:T(8,128)(4,1)S(1)} %copy-done.8), kind=kLoop, calls=%fused_computation.3 | loop fusion | flops 43253760 | bytes 108359680 | tf_op jit(solution)/shard_map/convert_element_type | solution.py:112
  (65 shorter events, 49.6 us)
Async XLA Ops:
  7.2 223.6 %copy-start = (bf16[192,512]{1,0:T(8,128)(2,1)S(1)}, bf16[192,512]{1,0:T(8,128)(2,1)}, u32[]{:S(2)}) copy-start(bf16[192,512]{1,0:T(8,128)(2,1)} %param.11) | copy-start | bytes 589828
  8.6 27.4 %copy-start.7 = (pred[80,1408]{1,0:T(8,128)(4,1)}, pred[80,1408]{1,0:T(8,128)(4,1)S(1)}, u32[]{:S(2)}) copy-start(pred[80,1408]{1,0:T(8,128)(4,1)S(1)} %get-tuple-element.20) | copy-start | bytes 337924
  8.6 27.4 %copy-start.9 = (pred[80,1408]{1,0:T(8,128)(4,1)}, pred[80,1408]{1,0:T(8,128)(4,1)S(1)}, u32[]{:S(2)}) copy-start(pred[80,1408]{1,0:T(8,128)(4,1)S(1)} %get-tuple-element.21) | copy-start | bytes 337924
  84.1 13.6 %copy-start.11 = (s32[640]{0:T(1024)S(1)}, s32[640]{0:T(1024)}, u32[]{:S(2)}) copy-start(s32[640]{0:T(1024)} %param.8) | copy-start | bytes 7684
  90.1 66.2 %all-to-all-start = ((bf16[160,8,768]{2,0,1:T(8,128)(2,1)}), bf16[160,8,768]{2,0,1:T(8,128)(2,1)S(1)}, u32[]{:S(2)}, u32[]{:S(2)}) async-start(bf16[160,8,768]{2,0,1:T(8,128)(2,1)} %copy.30), calls=%async_computation | async-start | bytes 3932160 | tf_op jit(solution)/shard_map/all_to_all | solution.py:64
  156.3 1.3 copy-start.2
  189.9 40.8 %copy-start.13 = (f32[512]{0:T(512)S(1)}, f32[512]{0:T(512)}, u32[]{:S(2)}) copy-start(f32[512]{0:T(512)} %param.12) | copy-start | bytes 6148
  230.8 5.5 %copy-start.6 = (bf16[8,48,4,640]{3,1,2,0:T(8,128)(2,1)}, bf16[8,48,4,640]{3,1,2,0:T(8,128)(2,1)S(1)}, u32[]{:S(2)}) copy-start(bf16[8,48,4,640]{3,1,2,0:T(8,128)(2,1)S(1)} %copy.35) | copy-start | bytes 5898244
  230.8 5.5 %copy-start.4 = (bf16[8,192,640]{2,1,0:T(8,128)(2,1)S(1)}, bf16[8,192,640]{2,1,0:T(8,128)(2,1)}, u32[]{:S(2)}) copy-start(bf16[8,192,640]{2,1,0:T(8,128)(2,1)} %param.15) | copy-start | bytes 5898244
  230.8 5.5 %copy-start.12 = (bf16[512,192]{0,1:T(8,128)(2,1)S(1)}, bf16[512,192]{0,1:T(8,128)(2,1)}, u32[]{:S(2)}) copy-start(bf16[512,192]{0,1:T(8,128)(2,1)} %param.13) | copy-start | bytes 589828
  245.0 31.4 %copy-start.3 = (bf16[8,640,512]{2,1,0:T(8,128)(2,1)}, bf16[8,640,512]{2,1,0:T(8,128)(2,1)S(1)}, u32[]{:S(2)}) copy-start(bf16[8,640,512]{2,1,0:T(8,128)(2,1)S(1)} %get-tuple-element.25) | copy-start | bytes 15728644
  300.1 59.3 %all-to-all-start.3 = ((bf16[8,160,768]{2,1,0:T(8,128)(2,1)}), bf16[8,160,768]{2,1,0:T(8,128)(2,1)S(1)}, u32[]{:S(2)}, u32[]{:S(2)}) async-start(bf16[8,160,768]{2,1,0:T(8,128)(2,1)} %copy.39), calls=%async_computation.3 | async-start | bytes 3932160 | tf_op jit(solution)/shard_map/all_to_all | solution.py:103
  306.1 53.3 %all-reduce.9.cloned.1.call-start = ((), (), s32[]{:S(2)}) async-start(), calls=%async_computation.5 | async-start | bytes 1572864 | tf_op jit(solution)/shard_map/psum | solution.py:96
  306.1 7.1 %copy-start.5 = (bf16[8,192,640]{2,1,0:T(8,128)(2,1)S(1)}, bf16[8,192,640]{2,1,0:T(8,128)(2,1)}, u32[]{:S(2)}) copy-start(bf16[8,192,640]{2,1,0:T(8,128)(2,1)} %param.15) | copy-start | bytes 5898244
  308.2 45.5 %copy-start.14 = (f32[192]{0:T(256)S(1)}, f32[192]{0:T(256)}, u32[]{:S(2)}) copy-start(f32[192]{0:T(256)} %param.14) | copy-start | bytes 2308
  317.7 121.5 %all-reduce.7.cloned.1.call-start = ((), (), s32[]{:S(2)}) async-start(), calls=%async_computation.4 | async-start | bytes 1572864 | tf_op jit(solution)/shard_map/psum | solution.py:95
  366.3 34.8 %copy-start.8 = (pred[80,1408]{1,0:T(8,128)(4,1)S(1)}, pred[80,1408]{1,0:T(8,128)(4,1)}, u32[]{:S(2)}) copy-start(pred[80,1408]{1,0:T(8,128)(4,1)} %copy-done.7) | copy-start | bytes 337924
  366.3 34.8 %copy-start.10 = (pred[80,1408]{1,0:T(8,128)(4,1)S(1)}, pred[80,1408]{1,0:T(8,128)(4,1)}, u32[]{:S(2)}) copy-start(pred[80,1408]{1,0:T(8,128)(4,1)} %copy-done.9) | copy-start | bytes 337924
  401.1 41.6 %copy-start.1 = (bf16[192,512]{1,0:T(8,128)(2,1)S(1)}, bf16[192,512]{1,0:T(8,128)(2,1)}, u32[]{:S(2)}) copy-start(bf16[192,512]{1,0:T(8,128)(2,1)} %param.11) | copy-start | bytes 589828
Sparse Core Ops, SparseCore 0:
  317.8 35.1 all-reduce.8
  359.5 79.5 all-reduce.6
